TPU v7x, 32 devices: a whole 2x2x4 slice. The times are simulated.
32 devices in a mesh: ctx: 2 (over x), tp: 4 (over y, core), dp: 4 (over z).
Axes of the slice: x: 2, y: 2, z: 4, core: 2. Of those that a mesh axis runs over, the one named last changes fastest.
Arguments:
- byte_embed: bfloat16 [8192, 1024], P(('dp', 'ctx', 'tp')), parts along dimension 0, may hold values from -6 to 6
- patch_start: int32 [8192], P(('dp', 'ctx', 'tp')), parts along dimension 0, may hold values from 0 to 1, as said below
- enc_gain: float32 [1024], replicated, may hold values from 0.1 to 1.9
- enc_qkv: bfloat16 [1024, 3072], replicated, may hold values from -4 to 4
- enc_out: bfloat16 [1024, 1024], replicated, may hold values from -0.1875 to 0.1875
- up_proj: bfloat16 [1024, 4096], P('ctx', 'tp'), may hold values from -0.1875 to 0.1875
- lat_gain: float32 [4096], replicated, may hold values from 0.1 to 1.9
- query_proj: bfloat16 [4096, 2048], P('ctx', 'tp'), may hold values from -4 to 4
- key_proj: bfloat16 [4096, 512], P('ctx', 'tp'), may hold values from -4 to 4
- value_matrix: bfloat16 [4096, 512], P('ctx', 'tp'), may hold values from -0.09375 to 0.09375
- out_proj: bfloat16 [2048, 4096], P('tp', 'ctx'), may hold values from -0.125 to 0.125
- down_proj: bfloat16 [4096, 1024], P('tp', 'ctx'), may hold values from -0.09375 to 0.09375
Outputs:
- byte_states: bfloat16 [8192, 1024], P(('dp', 'ctx', 'tp')), parts along dimension 0
There are 4 independent parts, one for each index of `dp`. A program takes and returns all parts, laid end to end along the dimension named above; an argument that names none is the same for every part. Nothing has to cross between parts.
Inputs may be any that keep to these rules, and one draw needn't show every extreme that they name: `patch_start`: byte 0 begins a patch; every patch spans 1 to 19 bytes; each aligned group of 1024 bytes holds at most 256 patch starts, and some group holds exactly 256.
All inputs are finite; a program needn't handle non-finite values.
Results may differ from a plain program's by a relative error of at most 0.015.
Values may be sent and summed in bfloat16 or wider, within the bound.
No kernel may reach another device: no remote copies, remote signals or barrier semaphores. Data moves between devices by JAX's collectives and lax.ppermute only.
A program may use at most 128 MiB of HBM per device.

v0:
```python
import jax
import jax.numpy as jnp
from jax import lax
from jax.sharding import PartitionSpec as P

BH = 16
HB = 64
HEAD_SIZE = 128
WIN = 512
EPS = 1e-05


def shifted(block, axis, distance):
    devices = range(lax.axis_size(axis))
    route = [(i - distance, i) for i in devices if i - distance in devices]
    return lax.ppermute(block, axis, route)


def rms_scale(values, gain):
    floats = values.astype(jnp.float32)
    return floats * lax.rsqrt(jnp.mean(floats * floats, axis=-1, keepdims=True) + EPS) * gain


def window_attend(query, keys, values, first):
    n_query = query.shape[0]
    n_key = keys.shape[0]
    qh = query.reshape(n_query, BH, HB)
    kh = keys.reshape(n_key, BH, HB)
    vh = values.reshape(n_key, BH, HB)
    scores = jnp.einsum("qhd,khd->hqk", qh, kh, preferred_element_type=jnp.float32) / jnp.sqrt(
        jnp.float32(HB)
    )
    q_pos = first + jnp.arange(n_query, dtype=jnp.int32)
    k_pos = first - (n_key - n_query) + jnp.arange(n_key, dtype=jnp.int32)
    allowed = (
        (k_pos[None, :] <= q_pos[:, None])
        & (k_pos[None, :] > q_pos[:, None] - WIN)
        & (k_pos[None, :] >= 0)
    )
    scores = jnp.where(allowed[None], scores, jnp.float32(-1e30))
    peak = jnp.max(scores, axis=-1, keepdims=True)
    expo = jnp.where(allowed[None], jnp.exp(scores - peak), jnp.float32(0.0))
    total = jnp.sum(expo, axis=-1, keepdims=True)
    mixed = (
        jnp.einsum(
            "hqk,khd->hqd", expo.astype(jnp.bfloat16), vh, preferred_element_type=jnp.float32
        )
        / total
    )
    return jnp.transpose(mixed, (1, 0, 2)).reshape(n_query, BH * HB).astype(jnp.bfloat16)


def local(
    byte_embed,
    patch_start,
    enc_gain,
    enc_qkv,
    enc_out,
    up_proj,
    lat_gain,
    query_proj,
    key_proj,
    value_matrix,
    out_proj,
    down_proj,
):
    nbytes = byte_embed.shape[0]
    width = byte_embed.shape[1]
    n_tp = lax.axis_size("tp")
    n_ctx = lax.axis_size("ctx")
    device = lax.axis_index(("ctx", "tp"))
    group = device // n_tp
    slots = n_tp * nbytes // 4
    normed = rms_scale(byte_embed, enc_gain).astype(jnp.bfloat16)
    qkv = jnp.dot(normed, enc_qkv, preferred_element_type=jnp.float32).astype(jnp.bfloat16)
    query = qkv[:, :width]
    earlier = (qkv[:, width : 2 * width], qkv[:, 2 * width :])
    key_list = [earlier[0]]
    value_list = [earlier[1]]
    for step in range(2):
        earlier = shifted((earlier[0], earlier[1]), ("ctx", "tp"), 1)
        key_list.insert(0, earlier[0])
        value_list.insert(0, earlier[1])
    context = window_attend(
        query,
        jnp.concatenate(key_list, axis=0),
        jnp.concatenate(value_list, axis=0),
        device * nbytes,
    )
    hidden = (
        byte_embed.astype(jnp.float32)
        + jnp.dot(context, enc_out, preferred_element_type=jnp.float32)
    ).astype(jnp.bfloat16)
    local_count = jnp.sum(patch_start)
    all_counts = lax.all_gather(local_count[None], ("ctx", "tp"), axis=0, tiled=True)
    before = jnp.cumsum(all_counts) - all_counts
    offset = before[device] - before[group * n_tp]
    group_counts = jnp.sum(all_counts.reshape(n_ctx, n_tp), axis=1)
    local_slot = jnp.cumsum(patch_start) - 1
    slot = offset + local_slot
    columns = jnp.arange(slots, dtype=jnp.int32)
    onehot = ((slot[:, None] == columns[None, :]) & (local_slot[:, None] >= 0)).astype(jnp.bfloat16)
    part_sum = jnp.dot(onehot.T, hidden, preferred_element_type=jnp.float32)
    part_count = jnp.sum(onehot.astype(jnp.float32), axis=0)
    leading = (local_slot < 0).astype(jnp.bfloat16)
    lead_sum = jnp.dot(leading[None, :], hidden, preferred_element_type=jnp.float32)
    lead_count = jnp.sum(leading.astype(jnp.float32))[None]
    recv_sum, recv_count = shifted((lead_sum, lead_count), ("ctx", "tp"), -1)
    last = offset + local_count - 1
    last_hot = (columns == last).astype(jnp.float32)
    part_sum = part_sum + last_hot[:, None] * recv_sum
    part_count = part_count + last_hot * recv_count
    sums, counts = (
        lax.psum_scatter(
            part_sum.astype(jnp.bfloat16), "tp", scatter_dimension=0, tiled=True
        ).astype(jnp.float32),
        lax.psum_scatter(
            part_count.astype(jnp.bfloat16), "tp", scatter_dimension=0, tiled=True
        ).astype(jnp.float32),
    )
    share = (sums / jnp.maximum(counts, 1.0)[:, None]).astype(jnp.bfloat16)
    pooled = lax.all_gather(share, "tp", axis=0, tiled=True)
    latent_part = jnp.dot(
        pooled,
        lax.all_gather(up_proj, "ctx", axis=0, tiled=True),
        preferred_element_type=jnp.float32,
    ).astype(jnp.bfloat16)
    latent = lax.all_gather(latent_part, "tp", axis=1, tiled=True)
    lnorm = rms_scale(latent, lat_gain).astype(jnp.bfloat16)

    def proj_add(piece):
        return jnp.dot(lnorm, piece, preferred_element_type=jnp.float32)

    q_sum = proj_add(lax.all_gather(query_proj, "ctx", axis=0, tiled=True))
    pieces = (
        lax.all_gather(key_proj, "ctx", axis=0, tiled=True),
        lax.all_gather(value_matrix, "ctx", axis=0, tiled=True),
    )
    k_sum, v_sum = tuple((proj_add(pieces[i]) for i in range(2)))
    q_local = q_sum.astype(jnp.bfloat16)
    k_local = k_sum.astype(jnp.bfloat16)
    v_local = v_sum.astype(jnp.bfloat16)
    heads_local = q_local.shape[1] // HEAD_SIZE
    kv_local = k_local.shape[1] // HEAD_SIZE
    share_count = heads_local // kv_local
    q_grouped = jnp.transpose(
        q_local.reshape(slots, kv_local, share_count, HEAD_SIZE), (1, 2, 0, 3)
    ).reshape(kv_local, share_count * slots, HEAD_SIZE)
    query_rows = group * slots + jnp.tile(jnp.arange(slots, dtype=jnp.int32), share_count)
    scale = 1.0 / jnp.sqrt(jnp.float32(HEAD_SIZE))
    peak = jnp.full((kv_local, share_count * slots), -1e30, jnp.float32)
    k_piece = lax.all_gather(k_local, "ctx", axis=0, tiled=True)
    v_piece = lax.all_gather(v_local, "ctx", axis=0, tiled=True)
    count = k_piece.shape[0]
    k_heads = jnp.transpose(k_piece.reshape(count, kv_local, HEAD_SIZE), (1, 0, 2))
    v_heads = jnp.transpose(v_piece.reshape(count, kv_local, HEAD_SIZE), (1, 0, 2))
    key_rows = jnp.arange(count, dtype=jnp.int32)
    used = key_rows % slots < group_counts[key_rows // slots]
    allowed = used[None, :] & (key_rows[None, :] <= query_rows[:, None])
    scores = (
        jnp.einsum("hqd,hkd->hqk", q_grouped, k_heads, preferred_element_type=jnp.float32) * scale
    )
    scores = jnp.where(allowed[None], scores, jnp.float32(-1e30))
    new_peak = jnp.maximum(peak, jnp.max(scores, axis=-1))
    expo = jnp.where(allowed[None], jnp.exp(scores - new_peak[..., None]), jnp.float32(0.0))
    total = jnp.sum(expo, axis=-1)
    accum = jnp.einsum(
        "hqk,hkd->hqd", expo.astype(jnp.bfloat16), v_heads, preferred_element_type=jnp.float32
    )
    peak, total, accum = (new_peak, total, accum)
    mixed = accum / total[..., None]
    attn = (
        jnp.transpose(mixed.reshape(kv_local, share_count, slots, HEAD_SIZE), (2, 0, 1, 3))
        .reshape(slots, heads_local * HEAD_SIZE)
        .astype(jnp.bfloat16)
    )
    partial_value = jnp.dot(
        attn,
        lax.all_gather(out_proj, "ctx", axis=1, tiled=True),
        preferred_element_type=jnp.float32,
    )
    attn_part = lax.psum_scatter(
        partial_value.astype(jnp.bfloat16), "tp", scatter_dimension=1, tiled=True
    ).astype(jnp.float32)
    latent_out = (latent_part.astype(jnp.float32) + attn_part).astype(jnp.bfloat16)
    down_part = jnp.dot(
        latent_out,
        lax.all_gather(down_proj, "ctx", axis=1, tiled=True),
        preferred_element_type=jnp.float32,
    )
    patch_out = lax.psum(down_part.astype(jnp.bfloat16), "tp")
    trailing = lax.dynamic_slice_in_dim(patch_out, last, 1, 0)
    carried = shifted(trailing, ("ctx", "tp"), 1)
    spread = jnp.dot(onehot, patch_out, preferred_element_type=jnp.float32) + leading.astype(
        jnp.float32
    )[:, None] * carried.astype(jnp.float32)
    return (hidden.astype(jnp.float32) + spread).astype(jnp.bfloat16)


def solution(mesh):
    placed = (
        P(("dp", "ctx", "tp"), None),
        P(("dp", "ctx", "tp")),
        P(),
        P(),
        P(),
        P("ctx", "tp"),
        P(),
        P("ctx", "tp"),
        P("ctx", "tp"),
        P("ctx", "tp"),
        P("tp", "ctx"),
        P("tp", "ctx"),
    )
    return jax.shard_map(
        local, mesh=mesh, in_specs=placed, out_specs=P(("dp", "ctx", "tp"), None), check_vma=False
    )
```

profile of v0, /device:TPU:2, one launch (start us, length us, event | category | flops | bytes accessed | tf_op | source)
XLA Modules:
  0.0 421.7 jit_solution(6950951048192426557)
XLA Ops:
  7.4 1.4 fusion.26
  8.8 4.9 %convolution_convert_fusion.1 = bf16[256,3072]{1,0:T(8,128)(2,1)S(1)} fusion(bf16[1024,3072]{1,0:T(8,128)(2,1)} %param.15, bf16[256,1024]{1,0:T(8,128)(2,1)} %param.12, f32[1024]{0:T(1024)} %param.14, f32[256]{0:T(256)S(1)} %add_rsqrt_fusion.1), kind=kOutput, calls=%fused_computation.15 | convolution fusion | flops 1612447744 | bytes 8393728 | tf_op jit(solution)/shard_map/dot_general | solution.py:75
  13.6 0.9 fusion.64
  14.6 1.9 collective-permute-start
  16.5 0.6 dynamic-slice
  17.1 0.6 reduce_sum.74
  17.7 1.3 dynamic-update-slice
  19.0 3.5 collective-permute-start.2
  22.5 7.2 %all-reduce = s32[8]{0:T(128)S(1)} all-reduce(s32[8]{0:T(128)S(1)} %dynamic-update-slice), channel_id=1, replica_groups=mesh['ctx'=2,'tp'=4,'dp'=4] {'ctx','tp'}, use_global_device_ids=true, to_apply=%add | all-reduce | flops 8 | bytes 64
  30.5 0.7 fusion.66
  32.5 2.4 collective-permute-start.1
  34.9 2.8 collective-permute-start.3
  38.3 1.0 copy.26
  39.5 6.8 %collective-permute-done.1 = bf16[256,1024]{1,0:T(8,128)(2,1)} collective-permute-done((bf16[256,1024]{1,0:T(8,128)(2,1)}, bf16[256,1024]{1,0:T(8,128)(2,1)}, u32[]{:S(2)}, u32[]{:S(2)}) %collective-permute-start.1) | collective-permute-done | bytes 524320 | tf_op jit(solution)/shard_map/ppermute | solution.py:16
  46.3 2.6 pad_maximum_fusion
  49.0 2.6 copy.27
  51.9 2.5 pad_maximum_fusion.1
  54.4 2.7 copy.28
  57.2 8.5 %fusion.67 = (f32[16,256]{1,0:T(8,128)S(1)}, bf16[16,256,768]{2,1,0:T(8,128)(2,1)}) fusion(pred[256,768]{1,0:T(8,128)(4,1)S(1)} %and_and_fusion, bf16[256,16,64]{0,2,1:T(8,128)(2,1)S(1)} %bitcast.72, bf16[768,16,64]{0,2,1:T(8,128)(2,1)} %bitcast.68), kind=kOutput, calls=%fused_computation.103 | convolution fusion | flops 421528320 | bytes 8601600 | tf_op jit(solution)/shard_map/sub | solution.py:42
  65.6 5.3 %fusion.23 = bf16[256,16,64]{0,2,1:T(8,128)(2,1)S(1)} fusion(bf16[768,16,64]{0,2,1:T(8,128)(2,1)} %bitcast.69, bf16[16,256,768]{2,1,0:T(8,128)(2,1)} %get-tuple-element.16, f32[256,16]{0,1:T(8,128)S(1)} %bitcast.82), kind=kOutput, calls=%fused_computation.36 | convolution fusion | flops 403177472 | bytes 8404992 | tf_op jit(solution)/shard_map/hqk,khd->hqd/dot_general | solution.py:45
  70.9 0.7 fusion.16
  71.9 1.9 collective-permute-start.4
  73.8 1.3 collective-permute-done.4
  75.1 1.2 add_convert_fusion.2
  77.0 0.7 convert_reduce_fusion.1
  77.7 4.5 %collective-permute-start.5 = (f32[1]{0:T(128)}, f32[1]{0:T(128)}, u32[]{:S(2)}, u32[]{:S(2)}) collective-permute-start(f32[1]{0:T(128)} %bitcast.17), channel_id=1, source_target_pairs={{4,0},{8,4},{12,8},{16,12},{20,16},{24,20},{28,24},{5,1},{9,5},{13... | collective-permute-start | bytes 20 | tf_op jit(solution)/shard_map/ppermute | solution.py:16
  82.2 0.6 dynamic-slice.1
  83.6 0.6 add_convert_fusion.4
  84.2 5.8 %all-reduce.1 = bf16[256]{0:T(256)(128)(2,1)S(1)} all-reduce(bf16[256]{0:T(256)(128)(2,1)S(1)} %add_convert_fusion.4), channel_id=3, replica_groups=mesh['ctx'=2,'tp'=4,'dp'=4] {'tp'}, use_global_device_ids=true, to_apply=%region_10.11.clone | all-reduce | flops 256 | bytes 1024
  90.1 9.6 %reduce-scatter.3.cloned.1.call-done = bf16[64,1024]{1,0:T(8,128)(2,1)} async-done(((bf16[256,1024]{1,0:T(8,128)(2,1)}), bf16[64,1024]{1,0:T(8,128)(2,1)}) %reduce-scatter.3.cloned.1.call-update) | async-done | bytes 131088 | tf_op jit(solution)/shard_map/reduce_scatter | solution.py:114
  99.7 1.0 divide_convert_fusion
  100.7 6.6 %all_gather.34 = bf16[256,1024]{1,0:T(8,128)(2,1)S(1)} all-gather(bf16[64,1024]{1,0:T(8,128)(2,1)S(1)} %divide_convert_fusion), channel_id=1, replica_groups=mesh['ctx'=2,'tp'=4,'dp'=4] {'tp'}, dimensions={0}, use_global_device_ids=true | all-gather | bytes 655360 | tf_op jit(solution)/shard_map/all_gather | solution.py:122
  107.3 4.4 %all-gather.8.cloned.1.call-done = bf16[1024,1024]{1,0:T(8,128)(2,1)} async-done(((bf16[512,1024]{1,0:T(8,128)(2,1)}), bf16[1024,1024]{1,0:T(8,128)(2,1)}) %all-gather.8.cloned.1.call-update) | async-done | bytes 2097168 | tf_op jit(solution)/shard_map/all_gather | solution.py:125
  111.7 3.1 convolution_convert_fusion.3
  114.8 0.7 all-gather.12.cloned.1.call-update
  115.6 0.5 all-gather.14.cloned.1.call-update
  116.1 0.5 all-gather.16.cloned.1.call-update
  116.7 0.5 all-gather.18.cloned.1.call-update
  117.3 0.7 all-gather.20.cloned.1.call-update
  118.5 0.6 fusion.65
  119.1 1.3 compare_select_fusion.1
  120.5 18.2 %all-gather.10.cloned.1.call-done = bf16[256,4096]{1,0:T(8,128)(2,1)} async-done(((bf16[256,1024]{1,0:T(8,128)(2,1)}), bf16[256,4096]{1,0:T(8,128)(2,1)}) %all-gather.10.cloned.1.call-update) | async-done | bytes 2097168 | tf_op jit(solution)/shard_map/all_gather | solution.py:128
  138.6 2.1 fusion.7
  140.7 55.1 %all-gather.12.cloned.1.call-done = bf16[4096,512]{1,0:T(8,128)(2,1)} async-done(((bf16[2048,512]{1,0:T(8,128)(2,1)}), bf16[4096,512]{1,0:T(8,128)(2,1)}) %all-gather.12.cloned.1.call-update) | async-done | bytes 4194320 | tf_op jit(solution)/shard_map/all_gather | solution.py:134
  195.8 4.1 convolution_convert_fusion.4
  200.0 18.5 %all-gather.14.cloned.1.call-done = bf16[4096,128]{1,0:T(8,128)(2,1)} async-done(((bf16[2048,128]{1,0:T(8,128)(2,1)}), bf16[4096,128]{1,0:T(8,128)(2,1)}) %all-gather.14.cloned.1.call-update) | async-done | bytes 1048592 | tf_op jit(solution)/shard_map/all_gather | solution.py:136
  218.5 2.7 convolution_convert_fusion.6
  221.2 4.9 %all_gather.39 = bf16[512,128]{1,0:T(8,128)(2,1)S(1)} all-gather(bf16[256,128]{1,0:T(8,128)(2,1)S(1)} %convolution_convert_fusion.6), channel_id=1, replica_groups=mesh['ctx'=2,'tp'=4,'dp'=4] {'ctx'}, dimensions={0}, use_global_device_ids=true | all-gather | bytes 196608 | tf_op jit(solution)/shard_map/all_gather | solution.py:152
  226.1 15.1 %all-gather.16.cloned.1.call-done = bf16[4096,128]{1,0:T(8,128)(2,1)} async-done(((bf16[2048,128]{1,0:T(8,128)(2,1)}), bf16[4096,128]{1,0:T(8,128)(2,1)}) %all-gather.16.cloned.1.call-update) | async-done | bytes 1048592 | tf_op jit(solution)/shard_map/all_gather | solution.py:137
  241.2 2.7 convolution_convert_fusion.5
  243.9 4.9 %all_gather.41 = bf16[512,128]{1,0:T(8,128)(2,1)S(1)} all-gather(bf16[256,128]{1,0:T(8,128)(2,1)S(1)} %convolution_convert_fusion.5), channel_id=1, replica_groups=mesh['ctx'=2,'tp'=4,'dp'=4] {'ctx'}, dimensions={0}, use_global_device_ids=true | all-gather | bytes 196608 | tf_op jit(solution)/shard_map/all_gather | solution.py:153
  248.8 0.7 fusion.68
  249.5 0.6 fusion.11
  250.2 0.9 fusion.19
  251.2 48.2 %all-gather.18.cloned.1.call-done = bf16[512,4096]{1,0:T(8,128)(2,1)} async-done(((bf16[512,2048]{1,0:T(8,128)(2,1)}), bf16[512,4096]{1,0:T(8,128)(2,1)}) %all-gather.18.cloned.1.call-update) | async-done | bytes 4194320 | tf_op jit(solution)/shard_map/all_gather | solution.py:179
  299.4 4.8 %convolution_convert_fusion = bf16[256,4096]{1,0:T(8,128)(2,1)} fusion(bf16[256,512]{0,1:T(8,128)(2,1)S(1)} %bitcast.70, bf16[512,4096]{1,0:T(8,128)(2,1)} %all-gather.18.cloned.1.call-done), kind=kOutput, calls=%fused_computation.11 | convolution fusion | flops 1074790400 | bytes 6553600 | tf_op jit(solution)/shard_map/dot_general | solution.py:177
  304.2 29.8 %all-gather.20.cloned.1.call-done = bf16[1024,1024]{1,0:T(8,128)(2,1)} async-done(((bf16[1024,512]{1,0:T(8,128)(2,1)}), bf16[1024,1024]{1,0:T(8,128)(2,1)}) %all-gather.20.cloned.1.call-update) | async-done | bytes 2097168 | tf_op jit(solution)/shard_map/all_gather | solution.py:188
  334.0 34.9 %reduce-scatter.5.cloned.1.call-done = bf16[256,1024]{1,0:T(8,128)(2,1)} async-done(((bf16[256,4096]{1,0:T(8,128)(2,1)}), bf16[256,1024]{1,0:T(8,128)(2,1)}) %reduce-scatter.5.cloned.1.call-update) | async-done | bytes 524304 | tf_op jit(solution)/shard_map/reduce_scatter | solution.py:182
  368.9 3.3 convolution_convert_fusion.2
  372.2 33.6 %all-reduce.4.cloned.1.call-done = bf16[256,1024]{1,0:T(8,128)(2,1)} async-done(((bf16[256,1024]{1,0:T(8,128)(2,1)}), bf16[256,1024]{1,0:T(8,128)(2,1)}) %all-reduce.4.cloned.1.call-update) | async-done | bytes 524304 | tf_op jit(solution)/shard_map/psum | solution.py:191
  405.8 0.7 constant_dynamic-slice_fusion
  406.5 1.9 collective-permute-start.6
  408.4 3.9 collective-permute-done.6
  412.3 2.2 add_convert_fusion
  (66 shorter events, 3.6 us)
Async XLA Ops:
  7.4 63.6 %copy-start = (bf16[1024,1024]{1,0:T(8,128)(2,1)S(1)}, bf16[1024,1024]{1,0:T(8,128)(2,1)}, u32[]{:S(2)}) copy-start(bf16[1024,1024]{1,0:T(8,128)(2,1)} %param.16) | copy-start | bytes 6291460
  7.4 92.3 %reduce-scatter.3.cloned.1.call-start = ((), (), s32[]{:S(2)}) async-start(), calls=%async_computation.2 | async-start | bytes 655360 | tf_op jit(solution)/shard_map/reduce_scatter | solution.py:114
  13.6 2.9 copy-start.7
  13.6 3.5 copy-start.4
  14.6 17.9 %collective-permute-start = (bf16[256,1024]{1,0:T(8,128)(2,1)}, bf16[256,1024]{1,0:T(8,128)(2,1)}, u32[]{:S(2)}, u32[]{:S(2)}) collective-permute-start(bf16[256,1024]{1,0:T(8,128)(2,1)} %get-tuple-element.8), channel_id=1, source_target_pairs={{0,4},{4,8},{8,12},{12,16},{16,20},{20,24},{24,28},{1,5},{5,9},{9,... | collective-permute-start | bytes 1572872 | tf_op jit(solution)/shard_map/ppermute | solution.py:16
  19.0 15.9 %collective-permute-start.2 = (bf16[256,1024]{1,0:T(8,128)(2,1)S(1)}, bf16[256,1024]{1,0:T(8,128)(2,1)}, u32[]{:S(2)}, u32[]{:S(2)}) collective-permute-start(bf16[256,1024]{1,0:T(8,128)(2,1)S(1)} %get-tuple-element.9), channel_id=1, source_target_pairs={{0,4},{4,8},{8,12},{12,16},{16,20},{20,24},{24,28},{1,5},{5,9},{9,... | collective-permute-start | bytes 1572872 | tf_op jit(solution)/shard_map/ppermute | solution.py:16
  32.5 13.9 %collective-permute-start.1 = (bf16[256,1024]{1,0:T(8,128)(2,1)}, bf16[256,1024]{1,0:T(8,128)(2,1)}, u32[]{:S(2)}, u32[]{:S(2)}) collective-permute-start(bf16[256,1024]{1,0:T(8,128)(2,1)} %collective-permute-done), channel_id=1, source_target_pairs={{0,4},{4,8},{8,12},{12,16},{16,20},{20,24},{24,28},{1,5},{5,9},{9,... | collective-permute-start | bytes 1572872 | tf_op jit(solution)/shard_map/ppermute | solution.py:16
  34.9 17.1 %collective-permute-start.3 = (bf16[256,1024]{1,0:T(8,128)(2,1)}, bf16[256,1024]{1,0:T(8,128)(2,1)}, u32[]{:S(2)}, u32[]{:S(2)}) collective-permute-start(bf16[256,1024]{1,0:T(8,128)(2,1)} %collective-permute-done.2), channel_id=1, source_target_pairs={{0,4},{4,8},{8,12},{12,16},{16,20},{20,24},{24,28},{1,5},{5,9},{9,... | collective-permute-start | bytes 1572872 | tf_op jit(solution)/shard_map/ppermute | solution.py:16
  54.4 2.7 copy-start.3
  65.6 5.3 %copy-start.1 = (bf16[256,1024]{1,0:T(8,128)(2,1)S(1)}, bf16[256,1024]{1,0:T(8,128)(2,1)}, u32[]{:S(2)}) copy-start(bf16[256,1024]{1,0:T(8,128)(2,1)} %param.12) | copy-start | bytes 1572868
  71.7 10.5 %copy-start.6 = (u32[32]{0:T(128)S(1)}, u32[32]{0:T(128)}, u32[]{:S(2)}) copy-start(u32[32]{0:T(128)} %constant.112) | copy-start | bytes 388
  71.9 3.2 collective-permute-start.4
  76.4 35.3 %all-gather.8.cloned.1.call-start = ((), (), s32[]{:S(2)}) async-start(), calls=%async_computation.3 | async-start | bytes 3145728 | tf_op jit(solution)/shard_map/all_gather | solution.py:125
  76.9 61.7 %all-gather.10.cloned.1.call-start = ((), (), s32[]{:S(2)}) async-start(), calls=%async_computation.4 | async-start | bytes 2621440 | tf_op jit(solution)/shard_map/all_gather | solution.py:128
  77.7 5.9 %collective-permute-start.5 = (f32[1]{0:T(128)}, f32[1]{0:T(128)}, u32[]{:S(2)}, u32[]{:S(2)}) collective-permute-start(f32[1]{0:T(128)} %bitcast.17), channel_id=1, source_target_pairs={{4,0},{8,4},{12,8},{16,12},{20,16},{24,20},{28,24},{5,1},{9,5},{13... | collective-permute-start | bytes 20 | tf_op jit(solution)/shard_map/ppermute | solution.py:16
  114.8 81.0 %all-gather.12.cloned.1.call-start = ((), (), s32[]{:S(2)}) async-start(), calls=%async_computation.5 | async-start | bytes 6291456 | tf_op jit(solution)/shard_map/all_gather | solution.py:134
  115.5 103.0 %all-gather.14.cloned.1.call-start = ((), (), s32[]{:S(2)}) async-start(), calls=%async_computation.6 | async-start | bytes 1572864 | tf_op jit(solution)/shard_map/all_gather | solution.py:136
  116.1 125.1 %all-gather.16.cloned.1.call-start = ((), (), s32[]{:S(2)}) async-start(), calls=%async_computation.7 | async-start | bytes 1572864 | tf_op jit(solution)/shard_map/all_gather | solution.py:137
  116.7 182.7 %all-gather.18.cloned.1.call-start = ((), (), s32[]{:S(2)}) async-start(), calls=%async_computation.8 | async-start | bytes 6291456 | tf_op jit(solution)/shard_map/all_gather | solution.py:179
  117.3 78.5 %copy-start.5 = (f32[4096]{0:T(1024)S(1)}, f32[4096]{0:T(1024)}, u32[]{:S(2)}) copy-start(f32[4096]{0:T(1024)} %param.18) | copy-start | bytes 49156
  117.3 216.8 %all-gather.20.cloned.1.call-start = ((), (), s32[]{:S(2)}) async-start(), calls=%async_computation.10 | async-start | bytes 3145728 | tf_op jit(solution)/shard_map/all_gather | solution.py:188
  118.0 250.9 %reduce-scatter.5.cloned.1.call-start = ((), (), s32[]{:S(2)}) async-start(), calls=%async_computation.9 | async-start | bytes 2621440 | tf_op jit(solution)/shard_map/reduce_scatter | solution.py:182
  304.2 64.7 %copy-start.2 = (bf16[256,1024]{1,0:T(8,128)(2,1)S(1)}, bf16[256,1024]{1,0:T(8,128)(2,1)}, u32[]{:S(2)}) copy-start(bf16[256,1024]{1,0:T(8,128)(2,1)} %convolution_convert_fusion.3) | copy-start | bytes 1572868
  304.2 101.6 %all-reduce.4.cloned.1.call-start = ((), (), s32[]{:S(2)}) async-start(), calls=%async_computation.11 | async-start | bytes 1048576 | tf_op jit(solution)/shard_map/psum | solution.py:191
  406.5 5.8 %collective-permute-start.6 = (bf16[1,1024]{1,0:T(2,128)(2,1)S(1)}, bf16[1,1024]{1,0:T(2,128)(2,1)S(1)}, u32[]{:S(2)}, u32[]{:S(2)}) collective-permute-start(bf16[1,1024]{1,0:T(2,128)(2,1)S(1)} %constant_dynamic-slice_fusion), channel_id=1, source_target_pairs={{0,4},{4,8},{8,12},{12,16},{16,20},{20,24},{24,28},{1,5},{5,9},{9,... | collective-permute-start | bytes 6152 | tf_op jit(solution)/shard_map/ppermute | solution.py:16
Sparse Core Ops, SparseCore 0:
  76.5 23.1 reduce-scatter.2
  114.9 23.6 all-gather.9
  140.2 55.5 all-gather.11
  197.2 21.2 all-gather.13
  219.9 21.2 all-gather.15
  242.6 56.7 all-gather.17
  300.9 33.0 all-gather.19
  336.6 32.2 reduce-scatter.4
  372.3 33.4 all-reduce.3
Sparse Core Ops, SparseCore 1:
  78.4 33.2 all-gather.7
where the time goes:
time: 422 us
  waiting for transfers between devices  283 us (67%)
  matrix products  45.1 us (11%)
  blocking collectives  29.4 us (7%)
  starting transfers between devices  19.5 us (5%)
  between operations  17.4 us (4%)
  other arithmetic  14.7 us (3%)
  local copies, waits for them, and re-layouts  12.3 us (3%)
    all_gather x1, waiting for transfers between devices, local(): q_sum = proj_add(lax.all_gather(query_proj, 'ctx', axis=0, tiled=True))  55.1 us
    all_gather x1, waiting for transfers between devices, local(): lax.all_gather(out_proj, 'ctx', axis=1, tiled=True)  48.2 us
    reduce_scatter x1, waiting for transfers between devices, local(): lax.psum_scatter(partial_value.astype(jnp.bfloat16), 'tp', scatter_dimens...  34.9 us
    psum x1, waiting for transfers between devices, local(): patch_out = lax.psum(down_part.astype(jnp.bfloat16), 'tp')  33.6 us
    all_gather x1, waiting for transfers between devices, local(): lax.all_gather(down_proj, 'ctx', axis=1, tiled=True)  29.8 us
    ppermute x7, starting transfers between devices, shifted(): return lax.ppermute(block, axis, route)  18.9 us
    all_gather x1, waiting for transfers between devices, local(): lax.all_gather(key_proj, 'ctx', axis=0, tiled=True)  18.5 us
    all_gather x1, waiting for transfers between devices, local(): latent = lax.all_gather(latent_part, 'tp', axis=1, tiled=True)  18.2 us
  transfers between devices with their start and end apart: 17, of which 14 were waited for; matrix products, arithmetic and copies ran while one was open for 8% of the time, Pallas kernels for 0%

commit v1 on v0

--- a/solution.py
+++ b/solution.py
@@ -149,8 +149,11 @@
     query_rows = group * slots + jnp.tile(jnp.arange(slots, dtype=jnp.int32), share_count)
     scale = 1.0 / jnp.sqrt(jnp.float32(HEAD_SIZE))
     peak = jnp.full((kv_local, share_count * slots), -1e30, jnp.float32)
-    k_piece = lax.all_gather(k_local, "ctx", axis=0, tiled=True)
-    v_piece = lax.all_gather(v_local, "ctx", axis=0, tiled=True)
+    k_piece, v_piece = jnp.split(
+        lax.all_gather(jnp.concatenate([k_local, v_local], axis=1), "ctx", axis=0, tiled=True),
+        [k_local.shape[1]],
+        axis=1,
+    )
     count = k_piece.shape[0]
     k_heads = jnp.transpose(k_piece.reshape(count, kv_local, HEAD_SIZE), (1, 0, 2))
     v_heads = jnp.transpose(v_piece.reshape(count, kv_local, HEAD_SIZE), (1, 0, 2))

time: 422 us -> 422 us (level)
    all_gather x1, waiting for transfers between devices: 15.1 us -> 19.8 us  [local(): lax.all_gather(value_matrix, 'ctx', axis=0, tiled=True)]
    all_gather x2 -> x1, blocking collectives: 9.87 us -> 5.92 us  [local(): lax.all_gather(jnp.concatenate([k_local, v_local], axis=1), 'ctx', axis=0...]
where the time goes in v1:
time: 422 us
  waiting for transfers between devices  287 us (68%)
  matrix products  45.5 us (11%)
  blocking collectives  25.5 us (6%)
  starting transfers between devices  19.5 us (5%)
  between operations  17.4 us (4%)
  other arithmetic  14.7 us (3%)
  local copies, waits for them, and re-layouts  12.3 us (3%)
    all_gather x1, waiting for transfers between devices, local(): q_sum = proj_add(lax.all_gather(query_proj, 'ctx', axis=0, tiled=True))  55.1 us
    all_gather x1, waiting for transfers between devices, local(): lax.all_gather(out_proj, 'ctx', axis=1, tiled=True)  46.9 us
    reduce_scatter x1, waiting for transfers between devices, local(): lax.psum_scatter(partial_value.astype(jnp.bfloat16), 'tp', scatter_dimens...  34.9 us
    psum x1, waiting for transfers between devices, local(): patch_out = lax.psum(down_part.astype(jnp.bfloat16), 'tp')  33.6 us
    all_gather x1, waiting for transfers between devices, local(): lax.all_gather(down_proj, 'ctx', axis=1, tiled=True)  29.8 us
    all_gather x1, waiting for transfers between devices, local(): lax.all_gather(value_matrix, 'ctx', axis=0, tiled=True)  19.8 us
    ppermute x7, starting transfers between devices, shifted(): return lax.ppermute(block, axis, route)  18.9 us
    all_gather x1, waiting for transfers between devices, local(): lax.all_gather(key_proj, 'ctx', axis=0, tiled=True)  18.6 us
  transfers between devices with their start and end apart: 17, of which 14 were waited for; matrix products, arithmetic and copies ran while one was open for 8% of the time, Pallas kernels for 0%

profile of v1, /device:TPU:2, one launch (start us, length us, event | category | flops | bytes accessed | tf_op | source)
XLA Modules:
  0.0 421.7 jit_solution(5062676175057190418)
XLA Ops:
  7.4 1.4 fusion.26
  8.8 4.9 %convolution_convert_fusion.1 = bf16[256,3072]{1,0:T(8,128)(2,1)S(1)} fusion(bf16[1024,3072]{1,0:T(8,128)(2,1)} %param.15, bf16[256,1024]{1,0:T(8,128)(2,1)} %param.12, f32[1024]{0:T(1024)} %param.14, f32[256]{0:T(256)S(1)} %add_rsqrt_fusion.1), kind=kOutput, calls=%fused_computation.15 | convolution fusion | flops 1612447744 | bytes 8393728 | tf_op jit(solution)/shard_map/dot_general | solution.py:75
  13.6 0.9 fusion.66
  14.6 1.9 collective-permute-start
  16.5 0.6 dynamic-slice
  17.1 0.6 reduce_sum.74
  17.7 1.3 dynamic-update-slice
  19.0 3.5 collective-permute-start.2
  22.5 7.2 %all-reduce = s32[8]{0:T(128)S(1)} all-reduce(s32[8]{0:T(128)S(1)} %dynamic-update-slice), channel_id=1, replica_groups=mesh['ctx'=2,'tp'=4,'dp'=4] {'ctx','tp'}, use_global_device_ids=true, to_apply=%add | all-reduce | flops 8 | bytes 64
  30.5 0.7 fusion.68
  32.5 2.4 collective-permute-start.1
  34.9 2.8 collective-permute-start.3
  38.3 1.0 copy.26
  39.5 6.8 %collective-permute-done.1 = bf16[256,1024]{1,0:T(8,128)(2,1)} collective-permute-done((bf16[256,1024]{1,0:T(8,128)(2,1)}, bf16[256,1024]{1,0:T(8,128)(2,1)}, u32[]{:S(2)}, u32[]{:S(2)}) %collective-permute-start.1) | collective-permute-done | bytes 524320 | tf_op jit(solution)/shard_map/ppermute | solution.py:16
  46.3 2.6 pad_maximum_fusion
  49.0 2.6 copy.27
  51.9 2.5 pad_maximum_fusion.1
  54.4 2.7 copy.28
  57.2 8.5 %fusion.69 = (f32[16,256]{1,0:T(8,128)S(1)}, bf16[16,256,768]{2,1,0:T(8,128)(2,1)}) fusion(pred[256,768]{1,0:T(8,128)(4,1)S(1)} %and_and_fusion, bf16[256,16,64]{0,2,1:T(8,128)(2,1)S(1)} %bitcast.70, bf16[768,16,64]{0,2,1:T(8,128)(2,1)} %bitcast.66), kind=kOutput, calls=%fused_computation.106 | convolution fusion | flops 421528320 | bytes 8601600 | tf_op jit(solution)/shard_map/sub | solution.py:42
  65.6 5.3 %fusion.23 = bf16[256,16,64]{0,2,1:T(8,128)(2,1)S(1)} fusion(bf16[768,16,64]{0,2,1:T(8,128)(2,1)} %bitcast.67, bf16[16,256,768]{2,1,0:T(8,128)(2,1)} %get-tuple-element.16, f32[256,16]{0,1:T(8,128)S(1)} %bitcast.80), kind=kOutput, calls=%fused_computation.36 | convolution fusion | flops 403177472 | bytes 8404992 | tf_op jit(solution)/shard_map/hqk,khd->hqd/dot_general | solution.py:45
  70.9 0.7 fusion.16
  71.9 1.9 collective-permute-start.4
  73.8 1.3 collective-permute-done.4
  75.1 1.2 add_convert_fusion.2
  76.4 0.5 all-gather.8.cloned.1.call-update
  77.0 0.7 convert_reduce_fusion.1
  77.7 4.5 %collective-permute-start.5 = (f32[1]{0:T(128)}, f32[1]{0:T(128)}, u32[]{:S(2)}, u32[]{:S(2)}) collective-permute-start(f32[1]{0:T(128)} %bitcast.17), channel_id=1, source_target_pairs={{4,0},{8,4},{12,8},{16,12},{20,16},{24,20},{28,24},{5,1},{9,5},{13... | collective-permute-start | bytes 20 | tf_op jit(solution)/shard_map/ppermute | solution.py:16
  82.2 0.6 dynamic-slice.1
  83.6 0.6 add_convert_fusion.4
  84.2 5.8 %all-reduce.1 = bf16[256]{0:T(256)(128)(2,1)S(1)} all-reduce(bf16[256]{0:T(256)(128)(2,1)S(1)} %add_convert_fusion.4), channel_id=3, replica_groups=mesh['ctx'=2,'tp'=4,'dp'=4] {'tp'}, use_global_device_ids=true, to_apply=%region_10.11.clone | all-reduce | flops 256 | bytes 1024
  90.1 9.6 %reduce-scatter.3.cloned.1.call-done = bf16[64,1024]{1,0:T(8,128)(2,1)} async-done(((bf16[256,1024]{1,0:T(8,128)(2,1)}), bf16[64,1024]{1,0:T(8,128)(2,1)}) %reduce-scatter.3.cloned.1.call-update) | async-done | bytes 131088 | tf_op jit(solution)/shard_map/reduce_scatter | solution.py:114
  99.7 1.0 divide_convert_fusion
  100.7 6.6 %all_gather.31 = bf16[256,1024]{1,0:T(8,128)(2,1)S(1)} all-gather(bf16[64,1024]{1,0:T(8,128)(2,1)S(1)} %divide_convert_fusion), channel_id=1, replica_groups=mesh['ctx'=2,'tp'=4,'dp'=4] {'tp'}, dimensions={0}, use_global_device_ids=true | all-gather | bytes 655360 | tf_op jit(solution)/shard_map/all_gather | solution.py:122
  107.3 4.4 %all-gather.8.cloned.1.call-done = bf16[1024,1024]{1,0:T(8,128)(2,1)} async-done(((bf16[512,1024]{1,0:T(8,128)(2,1)}), bf16[1024,1024]{1,0:T(8,128)(2,1)}) %all-gather.8.cloned.1.call-update) | async-done | bytes 2097168 | tf_op jit(solution)/shard_map/all_gather | solution.py:125
  111.7 3.1 convolution_convert_fusion.3
  114.8 0.7 all-gather.12.cloned.1.call-update
  115.6 0.5 all-gather.14.cloned.1.call-update
  116.1 0.5 all-gather.16.cloned.1.call-update
  116.7 0.5 all-gather.18.cloned.1.call-update
  117.3 0.7 all-gather.20.cloned.1.call-update
  118.5 0.6 fusion.67
  119.1 1.3 compare_select_fusion.1
  120.5 18.2 %all-gather.10.cloned.1.call-done = bf16[256,4096]{1,0:T(8,128)(2,1)} async-done(((bf16[256,1024]{1,0:T(8,128)(2,1)}), bf16[256,4096]{1,0:T(8,128)(2,1)}) %all-gather.10.cloned.1.call-update) | async-done | bytes 2097168 | tf_op jit(solution)/shard_map/all_gather | solution.py:128
  138.6 2.1 fusion.7
  140.7 55.1 %all-gather.12.cloned.1.call-done = bf16[4096,512]{1,0:T(8,128)(2,1)} async-done(((bf16[2048,512]{1,0:T(8,128)(2,1)}), bf16[4096,512]{1,0:T(8,128)(2,1)}) %all-gather.12.cloned.1.call-update) | async-done | bytes 4194320 | tf_op jit(solution)/shard_map/all_gather | solution.py:134
  195.8 4.1 convolution_convert_fusion.4
  199.9 18.6 %all-gather.14.cloned.1.call-done = bf16[4096,128]{1,0:T(8,128)(2,1)} async-done(((bf16[2048,128]{1,0:T(8,128)(2,1)}), bf16[4096,128]{1,0:T(8,128)(2,1)}) %all-gather.14.cloned.1.call-update) | async-done | bytes 1048592 | tf_op jit(solution)/shard_map/all_gather | solution.py:136
  218.5 2.8 convolution_convert_fusion.6
  221.5 19.8 %all-gather.16.cloned.1.call-done = bf16[4096,128]{1,0:T(8,128)(2,1)} async-done(((bf16[2048,128]{1,0:T(8,128)(2,1)}), bf16[4096,128]{1,0:T(8,128)(2,1)}) %all-gather.16.cloned.1.call-update) | async-done | bytes 1048592 | tf_op jit(solution)/shard_map/all_gather | solution.py:137
  241.2 2.8 convolution_convert_fusion.5
  244.1 5.9 %all_gather.37 = bf16[512,256]{0,1:T(8,128)(2,1)S(1)} all-gather(bf16[256,256]{0,1:T(8,128)(2,1)S(1)} %pad_maximum_fusion.2), channel_id=1, replica_groups=mesh['ctx'=2,'tp'=4,'dp'=4] {'ctx'}, dimensions={0}, use_global_device_ids=true | all-gather | bytes 393216 | tf_op jit(solution)/shard_map/all_gather | solution.py:153
  250.0 0.7 fusion.70
  250.7 0.6 fusion.11
  251.4 0.9 fusion.19
  252.4 46.9 %all-gather.18.cloned.1.call-done = bf16[512,4096]{1,0:T(8,128)(2,1)} async-done(((bf16[512,2048]{1,0:T(8,128)(2,1)}), bf16[512,4096]{1,0:T(8,128)(2,1)}) %all-gather.18.cloned.1.call-update) | async-done | bytes 4194320 | tf_op jit(solution)/shard_map/all_gather | solution.py:182
  299.4 4.8 %convolution_convert_fusion = bf16[256,4096]{1,0:T(8,128)(2,1)} fusion(bf16[256,512]{0,1:T(8,128)(2,1)S(1)} %bitcast.68, bf16[512,4096]{1,0:T(8,128)(2,1)} %all-gather.18.cloned.1.call-done), kind=kOutput, calls=%fused_computation.11 | convolution fusion | flops 1074790400 | bytes 6553600 | tf_op jit(solution)/shard_map/dot_general | solution.py:180
  304.2 29.8 %all-gather.20.cloned.1.call-done = bf16[1024,1024]{1,0:T(8,128)(2,1)} async-done(((bf16[1024,512]{1,0:T(8,128)(2,1)}), bf16[1024,1024]{1,0:T(8,128)(2,1)}) %all-gather.20.cloned.1.call-update) | async-done | bytes 2097168 | tf_op jit(solution)/shard_map/all_gather | solution.py:191
  334.0 34.9 %reduce-scatter.5.cloned.1.call-done = bf16[256,1024]{1,0:T(8,128)(2,1)} async-done(((bf16[256,4096]{1,0:T(8,128)(2,1)}), bf16[256,1024]{1,0:T(8,128)(2,1)}) %reduce-scatter.5.cloned.1.call-update) | async-done | bytes 524304 | tf_op jit(solution)/shard_map/reduce_scatter | solution.py:185
  368.9 3.3 convolution_convert_fusion.2
  372.2 33.6 %all-reduce.4.cloned.1.call-done = bf16[256,1024]{1,0:T(8,128)(2,1)} async-done(((bf16[256,1024]{1,0:T(8,128)(2,1)}), bf16[256,1024]{1,0:T(8,128)(2,1)}) %all-reduce.4.cloned.1.call-update) | async-done | bytes 524304 | tf_op jit(solution)/shard_map/psum | solution.py:194
  405.8 0.7 constant_dynamic-slice_fusion
  406.5 1.9 collective-permute-start.6
  408.4 3.9 collective-permute-done.6
  412.3 2.2 add_convert_fusion
  (66 shorter events, 3.1 us)
Async XLA Ops:
  7.4 63.6 %copy-start = (bf16[1024,1024]{1,0:T(8,128)(2,1)S(1)}, bf16[1024,1024]{1,0:T(8,128)(2,1)}, u32[]{:S(2)}) copy-start(bf16[1024,1024]{1,0:T(8,128)(2,1)} %param.16) | copy-start | bytes 6291460
  7.4 92.3 %reduce-scatter.3.cloned.1.call-start = ((), (), s32[]{:S(2)}) async-start(), calls=%async_computation.2 | async-start | bytes 655360 | tf_op jit(solution)/shard_map/reduce_scatter | solution.py:114
  13.6 2.9 copy-start.7
  13.6 3.5 copy-start.4
  14.6 17.9 %collective-permute-start = (bf16[256,1024]{1,0:T(8,128)(2,1)}, bf16[256,1024]{1,0:T(8,128)(2,1)}, u32[]{:S(2)}, u32[]{:S(2)}) collective-permute-start(bf16[256,1024]{1,0:T(8,128)(2,1)} %get-tuple-element.8), channel_id=1, source_target_pairs={{0,4},{4,8},{8,12},{12,16},{16,20},{20,24},{24,28},{1,5},{5,9},{9,... | collective-permute-start | bytes 1572872 | tf_op jit(solution)/shard_map/ppermute | solution.py:16
  19.0 15.9 %collective-permute-start.2 = (bf16[256,1024]{1,0:T(8,128)(2,1)S(1)}, bf16[256,1024]{1,0:T(8,128)(2,1)}, u32[]{:S(2)}, u32[]{:S(2)}) collective-permute-start(bf16[256,1024]{1,0:T(8,128)(2,1)S(1)} %get-tuple-element.9), channel_id=1, source_target_pairs={{0,4},{4,8},{8,12},{12,16},{16,20},{20,24},{24,28},{1,5},{5,9},{9,... | collective-permute-start | bytes 1572872 | tf_op jit(solution)/shard_map/ppermute | solution.py:16
  32.5 13.9 %collective-permute-start.1 = (bf16[256,1024]{1,0:T(8,128)(2,1)}, bf16[256,1024]{1,0:T(8,128)(2,1)}, u32[]{:S(2)}, u32[]{:S(2)}) collective-permute-start(bf16[256,1024]{1,0:T(8,128)(2,1)} %collective-permute-done), channel_id=1, source_target_pairs={{0,4},{4,8},{8,12},{12,16},{16,20},{20,24},{24,28},{1,5},{5,9},{9,... | collective-permute-start | bytes 1572872 | tf_op jit(solution)/shard_map/ppermute | solution.py:16
  34.9 17.1 %collective-permute-start.3 = (bf16[256,1024]{1,0:T(8,128)(2,1)}, bf16[256,1024]{1,0:T(8,128)(2,1)}, u32[]{:S(2)}, u32[]{:S(2)}) collective-permute-start(bf16[256,1024]{1,0:T(8,128)(2,1)} %collective-permute-done.2), channel_id=1, source_target_pairs={{0,4},{4,8},{8,12},{12,16},{16,20},{20,24},{24,28},{1,5},{5,9},{9,... | collective-permute-start | bytes 1572872 | tf_op jit(solution)/shard_map/ppermute | solution.py:16
  54.4 2.7 copy-start.3
  65.6 5.3 %copy-start.1 = (bf16[256,1024]{1,0:T(8,128)(2,1)S(1)}, bf16[256,1024]{1,0:T(8,128)(2,1)}, u32[]{:S(2)}) copy-start(bf16[256,1024]{1,0:T(8,128)(2,1)} %param.12) | copy-start | bytes 1572868
  71.7 10.5 %copy-start.6 = (u32[32]{0:T(128)S(1)}, u32[32]{0:T(128)}, u32[]{:S(2)}) copy-start(u32[32]{0:T(128)} %constant.112) | copy-start | bytes 388
  71.9 3.2 collective-permute-start.4
  76.4 35.3 %all-gather.8.cloned.1.call-start = ((), (), s32[]{:S(2)}) async-start(), calls=%async_computation.3 | async-start | bytes 3145728 | tf_op jit(solution)/shard_map/all_gather | solution.py:125
  76.9 61.7 %all-gather.10.cloned.1.call-start = ((), (), s32[]{:S(2)}) async-start(), calls=%async_computation.4 | async-start | bytes 2621440 | tf_op jit(solution)/shard_map/all_gather | solution.py:128
  77.7 5.9 %collective-permute-start.5 = (f32[1]{0:T(128)}, f32[1]{0:T(128)}, u32[]{:S(2)}, u32[]{:S(2)}) collective-permute-start(f32[1]{0:T(128)} %bitcast.17), channel_id=1, source_target_pairs={{4,0},{8,4},{12,8},{16,12},{20,16},{24,20},{28,24},{5,1},{9,5},{13... | collective-permute-start | bytes 20 | tf_op jit(solution)/shard_map/ppermute | solution.py:16
  114.8 81.0 %all-gather.12.cloned.1.call-start = ((), (), s32[]{:S(2)}) async-start(), calls=%async_computation.5 | async-start | bytes 6291456 | tf_op jit(solution)/shard_map/all_gather | solution.py:134
  115.5 103.0 %all-gather.14.cloned.1.call-start = ((), (), s32[]{:S(2)}) async-start(), calls=%async_computation.6 | async-start | bytes 1572864 | tf_op jit(solution)/shard_map/all_gather | solution.py:136
  116.1 125.1 %all-gather.16.cloned.1.call-start = ((), (), s32[]{:S(2)}) async-start(), calls=%async_computation.7 | async-start | bytes 1572864 | tf_op jit(solution)/shard_map/all_gather | solution.py:137
  116.7 182.7 %all-gather.18.cloned.1.call-start = ((), (), s32[]{:S(2)}) async-start(), calls=%async_computation.8 | async-start | bytes 6291456 | tf_op jit(solution)/shard_map/all_gather | solution.py:182
  117.3 78.5 %copy-start.5 = (f32[4096]{0:T(1024)S(1)}, f32[4096]{0:T(1024)}, u32[]{:S(2)}) copy-start(f32[4096]{0:T(1024)} %param.18) | copy-start | bytes 49156
  117.3 216.8 %all-gather.20.cloned.1.call-start = ((), (), s32[]{:S(2)}) async-start(), calls=%async_computation.10 | async-start | bytes 3145728 | tf_op jit(solution)/shard_map/all_gather | solution.py:191
  118.0 250.9 %reduce-scatter.5.cloned.1.call-start = ((), (), s32[]{:S(2)}) async-start(), calls=%async_computation.9 | async-start | bytes 2621440 | tf_op jit(solution)/shard_map/reduce_scatter | solution.py:185
  304.2 64.7 %copy-start.2 = (bf16[256,1024]{1,0:T(8,128)(2,1)S(1)}, bf16[256,1024]{1,0:T(8,128)(2,1)}, u32[]{:S(2)}) copy-start(bf16[256,1024]{1,0:T(8,128)(2,1)} %convolution_convert_fusion.3) | copy-start | bytes 1572868
  304.2 101.6 %all-reduce.4.cloned.1.call-start = ((), (), s32[]{:S(2)}) async-start(), calls=%async_computation.11 | async-start | bytes 1048576 | tf_op jit(solution)/shard_map/psum | solution.py:194
  406.5 5.8 %collective-permute-start.6 = (bf16[1,1024]{1,0:T(2,128)(2,1)S(1)}, bf16[1,1024]{1,0:T(2,128)(2,1)S(1)}, u32[]{:S(2)}, u32[]{:S(2)}) collective-permute-start(bf16[1,1024]{1,0:T(2,128)(2,1)S(1)} %constant_dynamic-slice_fusion), channel_id=1, source_target_pairs={{0,4},{4,8},{8,12},{12,16},{16,20},{20,24},{24,28},{1,5},{5,9},{9,... | collective-permute-start | bytes 6152 | tf_op jit(solution)/shard_map/ppermute | solution.py:16
Sparse Core Ops, SparseCore 0:
  76.5 23.1 reduce-scatter.2
  114.9 23.6 all-gather.9
  140.2 55.5 all-gather.11
  197.2 21.2 all-gather.13
  219.9 21.2 all-gather.15
  242.6 56.7 all-gather.17
  300.9 33.0 all-gather.19
  336.6 32.2 reduce-scatter.4
  372.3 33.4 all-reduce.3
Sparse Core Ops, SparseCore 1:
  78.4 33.2 all-gather.7
